TPU v7x, 32 devices: a whole 2x2x4 slice. The times are simulated.
32 devices in a mesh: section: 4 (over y, core), ep: 8 (over z, x).
Axes of the slice: x: 2, y: 2, z: 4, core: 2. Of those that a mesh axis runs over, the one named last changes fastest.
Arguments:
- rows_in: bfloat16 [4, 64, 7168], P(None, 'ep'), may hold values from -6 to 6
- routes: int32 [4, 4, 64, 2], P('section', None, 'ep'), may hold values from 0 to 3, all different within a row; in each aligned block of 8 rows (0 to 7, 8 to 15, ..., all dimensions but the last counted through in order) at most 4 rows name the same one
- hot_blocks: int32 [4], P('section'), may hold values from 0 to 15
- gains: float32 [4, 7168], P('section'), may hold values from 0.1 to 1.9
- router: bfloat16 [4, 7168, 4], P('section'), may hold values from -0.0625 to 0.0625
- w_gate: bfloat16 [4, 7168, 4096], P('section', None, 'ep'), may hold values from -0.0625 to 0.0625
- w_up: bfloat16 [4, 7168, 4096], P('section', None, 'ep'), may hold values from -0.0625 to 0.0625
- w_down: bfloat16 [4, 4096, 7168], P('section', 'ep'), may hold values from -0.1875 to 0.1875
Outputs:
- section_rows: bfloat16 [4, 4, 64, 7168], P('section', None, 'ep')
- relative_load: float32 [4, 8], P('section', 'ep')
Inputs may be any that keep to these rules, and one draw needn't show every extreme that they name: `routes`: in every layer and micro-batch the 8 rows of one device name each expert at most 4 times.
All inputs are finite; a program needn't handle non-finite values.
Results may differ from a plain program's by a relative error of at most 0.025.
Values may be sent and summed in bfloat16 or wider, within the bound.
A program may use at most 128 MiB of HBM per device.

v0:
```python
import jax
import jax.numpy as jnp
from jax import lax
from jax.sharding import PartitionSpec as P

FFW = 1024
BLK = 256


def shifted(block, axis, distance):
    devices = range(lax.axis_size(axis))
    route = [(i - distance, i) for i in devices if i - distance in devices]
    return lax.ppermute(block, axis, route)


def local(rows_in, routes, hot_blocks, gains, router, w_gate, w_up, w_down):
    section_index = lax.axis_index("section")
    ep_index = lax.axis_index("ep")
    section_count = lax.axis_size("section")
    micro_count = rows_in.shape[0]
    tok_rows = rows_in.shape[1]
    model_width = rows_in.shape[2]
    expert_count = router.shape[2]
    top_count = routes.shape[3]
    capacity = tok_rows // 2
    blocks_per_expert = FFW // BLK
    hot_index = hot_blocks[0]
    owner_index = hot_index // 2
    hot_expert = hot_index // blocks_per_expert
    norm_gain = gains[0]
    router_w = router[0]
    gate_w = w_gate[0]
    up_w = w_up[0]
    down_w = w_down[0]
    expert_ids = lax.iota(jnp.int32, expert_count)
    route_member = (routes[0][..., None] == expert_ids).astype(jnp.float32)
    expert_local = jnp.sum(route_member, axis=(0, 1, 2))
    expert_total = lax.psum(expert_local, "ep")
    own_expert = ep_index // 2
    home_units = jnp.sum(jnp.where(expert_ids == own_expert, expert_total, 0.0))
    own_hot = jnp.sum(jnp.where(expert_ids == hot_expert, expert_local, 0.0))

    def expert_rows(flat_rows):
        gate_value = jnp.dot(flat_rows, gate_w, preferred_element_type=jnp.float32)
        up_value = jnp.dot(flat_rows, up_w, preferred_element_type=jnp.float32)
        activation = (jax.nn.silu(gate_value) * up_value).astype(jnp.bfloat16)
        return jnp.dot(activation, down_w, preferred_element_type=jnp.float32).astype(jnp.bfloat16)

    def apply_layer(layer_input, route_ids):
        rows_float = layer_input.astype(jnp.float32)
        mean_square = jnp.mean(rows_float * rows_float, axis=-1, keepdims=True)
        normed = (rows_float * lax.rsqrt(mean_square + 1e-06) * norm_gain).astype(jnp.bfloat16)
        scores = jax.nn.sigmoid(jnp.dot(normed, router_w, preferred_element_type=jnp.float32))
        member = (route_ids[..., None] == expert_ids).astype(jnp.float32)
        chosen = jnp.sum(member * scores[:, :, None, :], axis=3)
        gate_weights = 2.5 * chosen / jnp.sum(chosen, axis=2, keepdims=True)
        token_gate = jnp.sum(member * gate_weights[..., None], axis=2)
        routed = jnp.sum(member, axis=2)
        slot_rank = jnp.cumsum(routed, axis=1) - routed
        slot_ids = lax.iota(jnp.float32, capacity)
        placement = jnp.swapaxes(routed, 1, 2)[:, :, None, :] * (
            jnp.swapaxes(slot_rank, 1, 2)[:, :, None, :] == slot_ids[None, None, :, None]
        ).astype(jnp.float32)
        packed = jnp.einsum(
            "mect,mtf->emcf",
            placement.astype(jnp.bfloat16),
            normed,
            preferred_element_type=jnp.float32,
        ).astype(jnp.bfloat16)
        packed = packed.reshape(expert_count, micro_count * capacity, model_width)
        send_rows = jnp.repeat(packed, 2, axis=0)
        recv_rows = lax.all_to_all(send_rows, "ep", split_axis=0, concat_axis=0, tiled=True)
        sources = recv_rows.shape[0]
        item_count = recv_rows.shape[1]
        part = expert_rows(recv_rows.reshape(sources * item_count, model_width))
        part = part.reshape(sources, item_count, model_width)
        home_back = lax.all_to_all(part, "ep", split_axis=0, concat_axis=0, tiled=True)
        combined = home_back.astype(jnp.float32).reshape(
            expert_count, 2, micro_count, capacity, model_width
        )
        pair_sum = combined[:, 0] + combined[:, 1]
        weighting = placement * jnp.swapaxes(token_gate, 1, 2)[:, :, None, :]
        routed_sum = jnp.einsum(
            "mect,emcf->mtf", weighting, pair_sum, precision=lax.Precision.HIGHEST
        )
        return (rows_float + routed_sum).astype(jnp.bfloat16)

    route_ids = routes[0]

    def run_step(step, loop_state):
        incoming, outputs = loop_state
        layer_input = jnp.where(section_index == 0, rows_in, incoming)
        next_rows = apply_layer(layer_input, route_ids)
        outputs = jnp.where(section_index == step, next_rows, outputs)
        return (shifted(next_rows, "section", 1), outputs)

    start_state = (jnp.zeros(rows_in.shape, jnp.bfloat16), jnp.zeros(rows_in.shape, jnp.bfloat16))
    outputs = lax.fori_loop(0, section_count, run_step, start_state)[1]
    unit_count = home_units * (2.0 - (owner_index == ep_index).astype(jnp.float32)) + own_hot
    relative = unit_count / float(micro_count * tok_rows * top_count * blocks_per_expert)
    return (outputs[None], relative.reshape(1, 1))


def solution(mesh):
    return jax.shard_map(
        local,
        mesh=mesh,
        in_specs=(
            P(None, "ep", None),
            P("section", None, "ep", None),
            P("section"),
            P("section", None),
            P("section", None, None),
            P("section", None, "ep"),
            P("section", None, "ep"),
            P("section", "ep", None),
        ),
        out_specs=(P("section", None, "ep", None), P("section", "ep")),
        check_vma=False,
    )
```

profile of v0, /device:TPU:1, one launch (start us, length us, event | category | flops | bytes accessed | tf_op | source)
XLA Modules:
  0.0 512.0 jit_solution(4193816347571856883)
XLA Ops:
  1.5 18.7 %psum.7 = f32[4]{0:T(128)S(1)} all-reduce(f32[4]{0:T(128)S(1)} %convert_reduce_fusion), channel_id=1, replica_groups=mesh['section'=4,'ep'=8] {'ep'}, use_global_device_ids=true, to_apply=%region_9.10 | all-reduce | flops 4 | bytes 32 | tf_op jit(solution)/shard_map/psum | solution.py:38
  24.1 486.0 %while.17 = (s32[]{:T(128)}, bf16[4,8,7168]{2,1,0:T(8,128)(2,1)S(1)}, bf16[4,8,7168]{2,1,0:T(8,128)(2,1)S(1)}, pred[]{:T(512)}, bf16[4,8,7168]{2,1,0:T(8,128)(2,...) while((s32[]{:T(128)}, ...), condition=%wide.region_7.8_spmd.clone, body=%wide.region_0.7_spmd.clone.sunk | while | flops 2877921280 | bytes 92975272 | solution.py:98
  29.0 43.1 %all_to_all.24 = bf16[8,16,7168]{2,1,0:T(8,128)(2,1)S(1)} all-to-all(bf16[8,16,7168]{2,1,0:T(8,128)(2,1)S(1)} %bitcast.91), channel_id=1, replica_groups=mesh['section'=4,'ep'=8] {'ep'}, dimensions={0} | all-to-all | bytes 3670016 | tf_op jit(solution)/shard_map/while/body/eval_jaxpr/all_to_all | solution.py:72
  73.2 8.6 %convolution_convert_fusion.3 = bf16[128,7168]{1,0:T(8,128)(2,1)} fusion(bf16[512,7168]{1,0:T(8,128)(2,1)} %get-tuple-element.493, bf16[128,7168]{1,0:T(8,128)(2,1)S(1)} %bitcast.86, bf16[7168,512]{1,0:T(8,128)(2,1)} %get-tuple-element.492, f32[128,512]{1,0:T(8,128)S(1)} %fusion.71), kind=kOutput, calls=%fused_computation.1.clone.1 | convolution fusion | flops 1880358912 | bytes 18612224 | tf_op jit(solution)/shard_map/while/body/eval_jaxpr/dot_general | solution.py:47
  81.9 4.1 all-to-all-start.1
  86.0 40.2 %all-to-all-done.1 = bf16[8,16,7168]{2,1,0:T(8,128)(2,1)S(1)} async-done(((bf16[8,16,7168]{2,1,0:T(8,128)(2,1)}), bf16[8,16,7168]{2,1,0:T(8,128)(2,1)S(1)}, u32[]{:S(2)}, u32[]{:S(2)}) %all-to-all-start.1) | async-done | bytes 1835040 | tf_op jit(solution)/shard_map/while/body/eval_jaxpr/all_to_all | solution.py:77
  126.2 2.4 reshape.91
  128.6 2.5 fusion.72
  131.1 3.7 select_select_fusion.2
  134.8 7.1 %collective-permute-start = (bf16[4,8,7168]{2,1,0:T(8,128)(2,1)S(1)}, bf16[4,8,7168]{2,1,0:T(8,128)(2,1)S(1)}, u32[]{:S(2)}, u32[]{:S(2)}) collective-permute-start(bf16[4,8,7168]{2,1,0:T(8,128)(2,1)S(1)} %get-tuple-element.451), channel_id=1, source_target_pairs={{0,8},{8,16},{16,24},{1,9},{9,17},{17,25},{2,10},{10,18},{18,26},{... | collective-permute-start | bytes 1376264 | tf_op jit(solution)/shard_map/while/body/eval_jaxpr/ppermute | solution.py:13
  141.9 5.4 %collective-permute-done = bf16[4,8,7168]{2,1,0:T(8,128)(2,1)S(1)} collective-permute-done((bf16[4,8,7168]{2,1,0:T(8,128)(2,1)S(1)}, bf16[4,8,7168]{2,1,0:T(8,128)(2,1)S(1)}, u32[]{:S(2)}, u32[]{:S(2)}) %collective-permute-start) | collective-permute-done | bytes 458784 | tf_op jit(solution)/shard_map/while/body/eval_jaxpr/ppermute | solution.py:13
  152.2 42.3 %all_to_all.24 = bf16[8,16,7168]{2,1,0:T(8,128)(2,1)S(1)} all-to-all(bf16[8,16,7168]{2,1,0:T(8,128)(2,1)S(1)} %bitcast.91), channel_id=1, replica_groups=mesh['section'=4,'ep'=8] {'ep'}, dimensions={0} | all-to-all | bytes 3670016 | tf_op jit(solution)/shard_map/while/body/eval_jaxpr/all_to_all | solution.py:72
  195.6 8.6 %convolution_convert_fusion.3 = bf16[128,7168]{1,0:T(8,128)(2,1)} fusion(bf16[512,7168]{1,0:T(8,128)(2,1)} %get-tuple-element.493, bf16[128,7168]{1,0:T(8,128)(2,1)S(1)} %bitcast.86, bf16[7168,512]{1,0:T(8,128)(2,1)} %get-tuple-element.492, f32[128,512]{1,0:T(8,128)S(1)} %fusion.71), kind=kOutput, calls=%fused_computation.1.clone.1 | convolution fusion | flops 1880358912 | bytes 18612224 | tf_op jit(solution)/shard_map/while/body/eval_jaxpr/dot_general | solution.py:47
  204.2 3.6 all-to-all-start.1
  207.8 43.3 %all-to-all-done.1 = bf16[8,16,7168]{2,1,0:T(8,128)(2,1)S(1)} async-done(((bf16[8,16,7168]{2,1,0:T(8,128)(2,1)}), bf16[8,16,7168]{2,1,0:T(8,128)(2,1)S(1)}, u32[]{:S(2)}, u32[]{:S(2)}) %all-to-all-start.1) | async-done | bytes 1835040 | tf_op jit(solution)/shard_map/while/body/eval_jaxpr/all_to_all | solution.py:77
  253.5 2.5 fusion.72
  256.0 3.7 select_select_fusion.2
  261.7 5.4 %collective-permute-done = bf16[4,8,7168]{2,1,0:T(8,128)(2,1)S(1)} collective-permute-done((bf16[4,8,7168]{2,1,0:T(8,128)(2,1)S(1)}, bf16[4,8,7168]{2,1,0:T(8,128)(2,1)S(1)}, u32[]{:S(2)}, u32[]{:S(2)}) %collective-permute-start) | collective-permute-done | bytes 458784 | tf_op jit(solution)/shard_map/while/body/eval_jaxpr/ppermute | solution.py:13
  271.9 44.4 %all_to_all.24 = bf16[8,16,7168]{2,1,0:T(8,128)(2,1)S(1)} all-to-all(bf16[8,16,7168]{2,1,0:T(8,128)(2,1)S(1)} %bitcast.91), channel_id=1, replica_groups=mesh['section'=4,'ep'=8] {'ep'}, dimensions={0} | all-to-all | bytes 3670016 | tf_op jit(solution)/shard_map/while/body/eval_jaxpr/all_to_all | solution.py:72
  317.4 8.6 %convolution_convert_fusion.3 = bf16[128,7168]{1,0:T(8,128)(2,1)} fusion(bf16[512,7168]{1,0:T(8,128)(2,1)} %get-tuple-element.493, bf16[128,7168]{1,0:T(8,128)(2,1)S(1)} %bitcast.86, bf16[7168,512]{1,0:T(8,128)(2,1)} %get-tuple-element.492, f32[128,512]{1,0:T(8,128)S(1)} %fusion.71), kind=kOutput, calls=%fused_computation.1.clone.1 | convolution fusion | flops 1880358912 | bytes 18612224 | tf_op jit(solution)/shard_map/while/body/eval_jaxpr/dot_general | solution.py:47
  326.1 3.6 all-to-all-start.1
  329.7 42.6 %all-to-all-done.1 = bf16[8,16,7168]{2,1,0:T(8,128)(2,1)S(1)} async-done(((bf16[8,16,7168]{2,1,0:T(8,128)(2,1)}), bf16[8,16,7168]{2,1,0:T(8,128)(2,1)S(1)}, u32[]{:S(2)}, u32[]{:S(2)}) %all-to-all-start.1) | async-done | bytes 1835040 | tf_op jit(solution)/shard_map/while/body/eval_jaxpr/all_to_all | solution.py:77
  374.7 2.5 fusion.72
  377.2 3.7 select_select_fusion.2
  382.8 5.4 %collective-permute-done = bf16[4,8,7168]{2,1,0:T(8,128)(2,1)S(1)} collective-permute-done((bf16[4,8,7168]{2,1,0:T(8,128)(2,1)S(1)}, bf16[4,8,7168]{2,1,0:T(8,128)(2,1)S(1)}, u32[]{:S(2)}, u32[]{:S(2)}) %collective-permute-start) | collective-permute-done | bytes 458784 | tf_op jit(solution)/shard_map/while/body/eval_jaxpr/ppermute | solution.py:13
  393.1 45.1 %all_to_all.24 = bf16[8,16,7168]{2,1,0:T(8,128)(2,1)S(1)} all-to-all(bf16[8,16,7168]{2,1,0:T(8,128)(2,1)S(1)} %bitcast.91), channel_id=1, replica_groups=mesh['section'=4,'ep'=8] {'ep'}, dimensions={0} | all-to-all | bytes 3670016 | tf_op jit(solution)/shard_map/while/body/eval_jaxpr/all_to_all | solution.py:72
  439.3 8.6 %convolution_convert_fusion.3 = bf16[128,7168]{1,0:T(8,128)(2,1)} fusion(bf16[512,7168]{1,0:T(8,128)(2,1)} %get-tuple-element.493, bf16[128,7168]{1,0:T(8,128)(2,1)S(1)} %bitcast.86, bf16[7168,512]{1,0:T(8,128)(2,1)} %get-tuple-element.492, f32[128,512]{1,0:T(8,128)S(1)} %fusion.71), kind=kOutput, calls=%fused_computation.1.clone.1 | convolution fusion | flops 1880358912 | bytes 18612224 | tf_op jit(solution)/shard_map/while/body/eval_jaxpr/dot_general | solution.py:47
  447.9 3.6 all-to-all-start.1
  451.5 42.6 %all-to-all-done.1 = bf16[8,16,7168]{2,1,0:T(8,128)(2,1)S(1)} async-done(((bf16[8,16,7168]{2,1,0:T(8,128)(2,1)}), bf16[8,16,7168]{2,1,0:T(8,128)(2,1)S(1)}, u32[]{:S(2)}, u32[]{:S(2)}) %all-to-all-start.1) | async-done | bytes 1835040 | tf_op jit(solution)/shard_map/while/body/eval_jaxpr/all_to_all | solution.py:77
  496.5 2.5 fusion.72
  499.1 3.7 select_select_fusion.2
  504.7 5.4 %collective-permute-done = bf16[4,8,7168]{2,1,0:T(8,128)(2,1)S(1)} collective-permute-done((bf16[4,8,7168]{2,1,0:T(8,128)(2,1)S(1)}, bf16[4,8,7168]{2,1,0:T(8,128)(2,1)S(1)}, u32[]{:S(2)}, u32[]{:S(2)}) %collective-permute-start) | collective-permute-done | bytes 458784 | tf_op jit(solution)/shard_map/while/body/eval_jaxpr/ppermute | solution.py:13
  (90 shorter events, 40.0 us)
Async XLA Ops:
  24.1 3.2 copy-start.2
  28.5 43.7 %copy-start = (bf16[7168,512]{1,0:T(8,128)(2,1)S(1)}, bf16[7168,512]{1,0:T(8,128)(2,1)}, u32[]{:S(2)}) copy-start(bf16[7168,512]{1,0:T(8,128)(2,1)} %get-tuple-element.491) | copy-start | bytes 22020100 | tf_op jit(solution)/shard_map/while
  81.9 44.3 %all-to-all-start.1 = ((bf16[8,16,7168]{2,1,0:T(8,128)(2,1)}), bf16[8,16,7168]{2,1,0:T(8,128)(2,1)S(1)}, u32[]{:S(2)}, u32[]{:S(2)}) async-start(bf16[8,16,7168]{2,1,0:T(8,128)(2,1)} %bitcast.88), calls=%async_computation.1 | async-start | bytes 3670016 | tf_op jit(solution)/shard_map/while/body/eval_jaxpr/all_to_all | solution.py:77
  134.8 12.5 %collective-permute-start = (bf16[4,8,7168]{2,1,0:T(8,128)(2,1)S(1)}, bf16[4,8,7168]{2,1,0:T(8,128)(2,1)S(1)}, u32[]{:S(2)}, u32[]{:S(2)}) collective-permute-start(bf16[4,8,7168]{2,1,0:T(8,128)(2,1)S(1)} %get-tuple-element.451), channel_id=1, source_target_pairs={{0,8},{8,16},{16,24},{1,9},{9,17},{17,25},{2,10},{10,18},{18,26},{... | collective-permute-start | bytes 1376264 | tf_op jit(solution)/shard_map/while/body/eval_jaxpr/ppermute | solution.py:13
  147.3 3.2 copy-start.2
  151.6 42.8 %copy-start = (bf16[7168,512]{1,0:T(8,128)(2,1)S(1)}, bf16[7168,512]{1,0:T(8,128)(2,1)}, u32[]{:S(2)}) copy-start(bf16[7168,512]{1,0:T(8,128)(2,1)} %get-tuple-element.491) | copy-start | bytes 22020100 | tf_op jit(solution)/shard_map/while
  204.2 46.9 %all-to-all-start.1 = ((bf16[8,16,7168]{2,1,0:T(8,128)(2,1)}), bf16[8,16,7168]{2,1,0:T(8,128)(2,1)S(1)}, u32[]{:S(2)}, u32[]{:S(2)}) async-start(bf16[8,16,7168]{2,1,0:T(8,128)(2,1)} %bitcast.88), calls=%async_computation.1 | async-start | bytes 3670016 | tf_op jit(solution)/shard_map/while/body/eval_jaxpr/all_to_all | solution.py:77
  259.8 7.3 %collective-permute-start = (bf16[4,8,7168]{2,1,0:T(8,128)(2,1)S(1)}, bf16[4,8,7168]{2,1,0:T(8,128)(2,1)S(1)}, u32[]{:S(2)}, u32[]{:S(2)}) collective-permute-start(bf16[4,8,7168]{2,1,0:T(8,128)(2,1)S(1)} %get-tuple-element.451), channel_id=1, source_target_pairs={{0,8},{8,16},{16,24},{1,9},{9,17},{17,25},{2,10},{10,18},{18,26},{... | collective-permute-start | bytes 1376264 | tf_op jit(solution)/shard_map/while/body/eval_jaxpr/ppermute | solution.py:13
  267.1 3.2 copy-start.2
  271.4 44.9 %copy-start = (bf16[7168,512]{1,0:T(8,128)(2,1)S(1)}, bf16[7168,512]{1,0:T(8,128)(2,1)}, u32[]{:S(2)}) copy-start(bf16[7168,512]{1,0:T(8,128)(2,1)} %get-tuple-element.491) | copy-start | bytes 22020100 | tf_op jit(solution)/shard_map/while
  326.1 46.2 %all-to-all-start.1 = ((bf16[8,16,7168]{2,1,0:T(8,128)(2,1)}), bf16[8,16,7168]{2,1,0:T(8,128)(2,1)S(1)}, u32[]{:S(2)}, u32[]{:S(2)}) async-start(bf16[8,16,7168]{2,1,0:T(8,128)(2,1)} %bitcast.88), calls=%async_computation.1 | async-start | bytes 3670016 | tf_op jit(solution)/shard_map/while/body/eval_jaxpr/all_to_all | solution.py:77
  380.9 7.3 %collective-permute-start = (bf16[4,8,7168]{2,1,0:T(8,128)(2,1)S(1)}, bf16[4,8,7168]{2,1,0:T(8,128)(2,1)S(1)}, u32[]{:S(2)}, u32[]{:S(2)}) collective-permute-start(bf16[4,8,7168]{2,1,0:T(8,128)(2,1)S(1)} %get-tuple-element.451), channel_id=1, source_target_pairs={{0,8},{8,16},{16,24},{1,9},{9,17},{17,25},{2,10},{10,18},{18,26},{... | collective-permute-start | bytes 1376264 | tf_op jit(solution)/shard_map/while/body/eval_jaxpr/ppermute | solution.py:13
  388.2 3.2 copy-start.2
  392.6 45.6 %copy-start = (bf16[7168,512]{1,0:T(8,128)(2,1)S(1)}, bf16[7168,512]{1,0:T(8,128)(2,1)}, u32[]{:S(2)}) copy-start(bf16[7168,512]{1,0:T(8,128)(2,1)} %get-tuple-element.491) | copy-start | bytes 22020100 | tf_op jit(solution)/shard_map/while
  447.9 46.2 %all-to-all-start.1 = ((bf16[8,16,7168]{2,1,0:T(8,128)(2,1)}), bf16[8,16,7168]{2,1,0:T(8,128)(2,1)S(1)}, u32[]{:S(2)}, u32[]{:S(2)}) async-start(bf16[8,16,7168]{2,1,0:T(8,128)(2,1)} %bitcast.88), calls=%async_computation.1 | async-start | bytes 3670016 | tf_op jit(solution)/shard_map/while/body/eval_jaxpr/all_to_all | solution.py:77
  502.8 7.3 %collective-permute-start = (bf16[4,8,7168]{2,1,0:T(8,128)(2,1)S(1)}, bf16[4,8,7168]{2,1,0:T(8,128)(2,1)S(1)}, u32[]{:S(2)}, u32[]{:S(2)}) collective-permute-start(bf16[4,8,7168]{2,1,0:T(8,128)(2,1)S(1)} %get-tuple-element.451), channel_id=1, source_target_pairs={{0,8},{8,16},{16,24},{1,9},{9,17},{17,25},{2,10},{10,18},{18,26},{... | collective-permute-start | bytes 1376264 | tf_op jit(solution)/shard_map/while/body/eval_jaxpr/ppermute | solution.py:13
  510.1 0.8 copy-start.1
where the time goes:
time: 513 us; the launch traced here: 512 us
  blocking collectives  194 us (38%)
  waiting for transfers between devices  190 us (37%)
  matrix products  64.8 us (13%)
  starting transfers between devices  27.7 us (5%)
  other arithmetic  16.5 us (3%)
  local copies, waits for them, and re-layouts  14.9 us (3%)
    all_to_all x4, blocking collectives, apply_layer(): lax.all_to_all(send_rows, 'ep', split_axis=0, concat_axis=0, tiled=True)  175 us
    all_to_all x4, waiting for transfers between devices, apply_layer(): lax.all_to_all(part, 'ep', split_axis=0, concat_axis=0, tiled=True)  169 us
    dot_general x4, matrix products, expert_rows(): jnp.dot(activation, down_w, preferred_element_type=jnp.float32)  34.6 us
    ppermute x4, waiting for transfers between devices, shifted(): return lax.ppermute(block, axis, route)  21.6 us
    psum x1, blocking collectives, local(): expert_total = lax.psum(expert_local, 'ep')  18.7 us
    all_to_all x4, starting transfers between devices, apply_layer(): lax.all_to_all(part, 'ep', split_axis=0, concat_axis=0, tiled=True)  14.9 us
    dot_general x4, matrix products, apply_layer(): jnp.einsum('mect,emcf->mtf', weighting, pair_sum, precision=lax.Precision...  14.9 us
    ppermute x4, starting transfers between devices, shifted(): return lax.ppermute(block, axis, route)  12.8 us
  transfers between devices with their start and end apart: 8, of which 8 were waited for; matrix products, arithmetic and copies ran while one was open for 0% of the time, Pallas kernels for 0%

commit v1 on v0

--- a/solution.py
+++ b/solution.py
@@ -35,7 +35,11 @@
     expert_ids = lax.iota(jnp.int32, expert_count)
     route_member = (routes[0][..., None] == expert_ids).astype(jnp.float32)
     expert_local = jnp.sum(route_member, axis=(0, 1, 2))
-    expert_total = lax.psum(expert_local, "ep")
+    expert_total = expert_local
+    for hop in (1, 2, 4):
+        expert_total = expert_total + lax.ppermute(
+            expert_total, "ep", [(dev, dev ^ hop) for dev in range(8)]
+        )
     own_expert = ep_index // 2
     home_units = jnp.sum(jnp.where(expert_ids == own_expert, expert_total, 0.0))
     own_hot = jnp.sum(jnp.where(expert_ids == hot_expert, expert_local, 0.0))

time: 513 us -> 505 us (0.984)
  blocking collectives: 194 us -> 177 us
  starting transfers between devices: 27.7 us -> 33.4 us
    psum x1 -> x0, blocking collectives: 18.7 us -> none  [local(): expert_total = lax.psum(expert_local, 'ep')]
    ppermute x0 -> x3, starting transfers between devices: none -> 5.69 us  [local(): lax.ppermute(expert_total, 'ep', [(dev, dev ^ hop) for dev in range(8)])]
  transfers between devices with their start and end apart: 8 -> 11, of which waited for: 8 -> 10; matrix products, arithmetic and copies ran while one was open for 0% -> 0% of each run, Pallas kernels for 0% -> 0%
where the time goes in v1:
time: 505 us; the launch traced here: 504 us
  waiting for transfers between devices  192 us (38%)
  blocking collectives  177 us (35%)
  matrix products  64.7 us (13%)
  starting transfers between devices  33.4 us (7%)
  other arithmetic  16.6 us (3%)
  local copies, waits for them, and re-layouts  14.9 us (3%)
    all_to_all x4, blocking collectives, apply_layer(): lax.all_to_all(send_rows, 'ep', split_axis=0, concat_axis=0, tiled=True)  177 us
    all_to_all x4, waiting for transfers between devices, apply_layer(): lax.all_to_all(part, 'ep', split_axis=0, concat_axis=0, tiled=True)  169 us
    dot_general x4, matrix products, expert_rows(): jnp.dot(activation, down_w, preferred_element_type=jnp.float32)  34.5 us
    ppermute x4, waiting for transfers between devices, shifted(): return lax.ppermute(block, axis, route)  21.6 us
    all_to_all x4, starting transfers between devices, apply_layer(): lax.all_to_all(part, 'ep', split_axis=0, concat_axis=0, tiled=True)  15 us
    dot_general x4, matrix products, apply_layer(): jnp.einsum('mect,emcf->mtf', weighting, pair_sum, precision=lax.Precision...  14.9 us
    ppermute x4, starting transfers between devices, shifted(): return lax.ppermute(block, axis, route)  12.8 us
    add x4, other arithmetic, apply_layer(): pair_sum = combined[:, 0] + combined[:, 1]  10.1 us
  transfers between devices with their start and end apart: 11, of which 10 were waited for; matrix products, arithmetic and copies ran while one was open for 0% of the time, Pallas kernels for 0%

profile of v1, /device:TPU:1, one launch (start us, length us, event | category | flops | bytes accessed | tf_op | source)
XLA Modules:
  0.0 503.8 jit_solution(15642452969657385796)
XLA Ops:
  13.3 488.6 %while.17 = (s32[]{:T(128)}, bf16[4,8,7168]{2,1,0:T(8,128)(2,1)S(1)}, bf16[4,8,7168]{2,1,0:T(8,128)(2,1)S(1)}, pred[]{:T(512)}, bf16[4,8,7168]{2,1,0:T(8,128)(2,...) while((s32[]{:T(128)}, ...), condition=%wide.region_7.8_spmd.clone, body=%wide.region_0.7_spmd.clone.sunk | while | flops 2877921280 | bytes 92975272 | solution.py:102
  18.2 45.7 %all_to_all.24 = bf16[8,16,7168]{2,1,0:T(8,128)(2,1)S(1)} all-to-all(bf16[8,16,7168]{2,1,0:T(8,128)(2,1)S(1)} %bitcast.91), channel_id=1, replica_groups=mesh['section'=4,'ep'=8] {'ep'}, dimensions={0} | all-to-all | bytes 3670016 | tf_op jit(solution)/shard_map/while/body/eval_jaxpr/all_to_all | solution.py:76
  65.0 8.6 %convolution_convert_fusion.3 = bf16[128,7168]{1,0:T(8,128)(2,1)} fusion(bf16[512,7168]{1,0:T(8,128)(2,1)} %get-tuple-element.495, bf16[128,7168]{1,0:T(8,128)(2,1)S(1)} %bitcast.86, bf16[7168,512]{1,0:T(8,128)(2,1)} %get-tuple-element.494, f32[128,512]{1,0:T(8,128)S(1)} %fusion.71), kind=kOutput, calls=%fused_computation.1.clone.1 | convolution fusion | flops 1880358912 | bytes 18612224 | tf_op jit(solution)/shard_map/while/body/eval_jaxpr/dot_general | solution.py:51
  73.6 4.2 all-to-all-start.1
  77.8 40.2 %all-to-all-done.1 = bf16[8,16,7168]{2,1,0:T(8,128)(2,1)S(1)} async-done(((bf16[8,16,7168]{2,1,0:T(8,128)(2,1)}), bf16[8,16,7168]{2,1,0:T(8,128)(2,1)S(1)}, u32[]{:S(2)}, u32[]{:S(2)}) %all-to-all-start.1) | async-done | bytes 1835040 | tf_op jit(solution)/shard_map/while/body/eval_jaxpr/all_to_all | solution.py:81
  118.1 2.4 reshape.91
  120.4 2.5 fusion.72
  123.0 3.7 select_select_fusion.2
  126.7 7.0 %collective-permute-start = (bf16[4,8,7168]{2,1,0:T(8,128)(2,1)S(1)}, bf16[4,8,7168]{2,1,0:T(8,128)(2,1)S(1)}, u32[]{:S(2)}, u32[]{:S(2)}) collective-permute-start(bf16[4,8,7168]{2,1,0:T(8,128)(2,1)S(1)} %get-tuple-element.453), channel_id=1, source_target_pairs={{0,8},{8,16},{16,24},{1,9},{9,17},{17,25},{2,10},{10,18},{18,26},{... | collective-permute-start | bytes 1376264 | tf_op jit(solution)/shard_map/while/body/eval_jaxpr/ppermute | solution.py:13
  133.7 5.4 %collective-permute-done = bf16[4,8,7168]{2,1,0:T(8,128)(2,1)S(1)} collective-permute-done((bf16[4,8,7168]{2,1,0:T(8,128)(2,1)S(1)}, bf16[4,8,7168]{2,1,0:T(8,128)(2,1)S(1)}, u32[]{:S(2)}, u32[]{:S(2)}) %collective-permute-start) | collective-permute-done | bytes 458784 | tf_op jit(solution)/shard_map/while/body/eval_jaxpr/ppermute | solution.py:13
  143.9 42.3 %all_to_all.24 = bf16[8,16,7168]{2,1,0:T(8,128)(2,1)S(1)} all-to-all(bf16[8,16,7168]{2,1,0:T(8,128)(2,1)S(1)} %bitcast.91), channel_id=1, replica_groups=mesh['section'=4,'ep'=8] {'ep'}, dimensions={0} | all-to-all | bytes 3670016 | tf_op jit(solution)/shard_map/while/body/eval_jaxpr/all_to_all | solution.py:76
  187.4 8.6 %convolution_convert_fusion.3 = bf16[128,7168]{1,0:T(8,128)(2,1)} fusion(bf16[512,7168]{1,0:T(8,128)(2,1)} %get-tuple-element.495, bf16[128,7168]{1,0:T(8,128)(2,1)S(1)} %bitcast.86, bf16[7168,512]{1,0:T(8,128)(2,1)} %get-tuple-element.494, f32[128,512]{1,0:T(8,128)S(1)} %fusion.71), kind=kOutput, calls=%fused_computation.1.clone.1 | convolution fusion | flops 1880358912 | bytes 18612224 | tf_op jit(solution)/shard_map/while/body/eval_jaxpr/dot_general | solution.py:51
  196.0 3.6 all-to-all-start.1
  199.6 43.3 %all-to-all-done.1 = bf16[8,16,7168]{2,1,0:T(8,128)(2,1)S(1)} async-done(((bf16[8,16,7168]{2,1,0:T(8,128)(2,1)}), bf16[8,16,7168]{2,1,0:T(8,128)(2,1)S(1)}, u32[]{:S(2)}, u32[]{:S(2)}) %all-to-all-start.1) | async-done | bytes 1835040 | tf_op jit(solution)/shard_map/while/body/eval_jaxpr/all_to_all | solution.py:81
  243.0 2.4 reshape.91
  245.3 2.5 fusion.72
  247.9 3.7 select_select_fusion.2
  253.5 5.4 %collective-permute-done = bf16[4,8,7168]{2,1,0:T(8,128)(2,1)S(1)} collective-permute-done((bf16[4,8,7168]{2,1,0:T(8,128)(2,1)S(1)}, bf16[4,8,7168]{2,1,0:T(8,128)(2,1)S(1)}, u32[]{:S(2)}, u32[]{:S(2)}) %collective-permute-start) | collective-permute-done | bytes 458784 | tf_op jit(solution)/shard_map/while/body/eval_jaxpr/ppermute | solution.py:13
  263.8 44.4 %all_to_all.24 = bf16[8,16,7168]{2,1,0:T(8,128)(2,1)S(1)} all-to-all(bf16[8,16,7168]{2,1,0:T(8,128)(2,1)S(1)} %bitcast.91), channel_id=1, replica_groups=mesh['section'=4,'ep'=8] {'ep'}, dimensions={0} | all-to-all | bytes 3670016 | tf_op jit(solution)/shard_map/while/body/eval_jaxpr/all_to_all | solution.py:76
  309.3 8.6 %convolution_convert_fusion.3 = bf16[128,7168]{1,0:T(8,128)(2,1)} fusion(bf16[512,7168]{1,0:T(8,128)(2,1)} %get-tuple-element.495, bf16[128,7168]{1,0:T(8,128)(2,1)S(1)} %bitcast.86, bf16[7168,512]{1,0:T(8,128)(2,1)} %get-tuple-element.494, f32[128,512]{1,0:T(8,128)S(1)} %fusion.71), kind=kOutput, calls=%fused_computation.1.clone.1 | convolution fusion | flops 1880358912 | bytes 18612224 | tf_op jit(solution)/shard_map/while/body/eval_jaxpr/dot_general | solution.py:51
  317.9 3.6 all-to-all-start.1
  321.5 42.6 %all-to-all-done.1 = bf16[8,16,7168]{2,1,0:T(8,128)(2,1)S(1)} async-done(((bf16[8,16,7168]{2,1,0:T(8,128)(2,1)}), bf16[8,16,7168]{2,1,0:T(8,128)(2,1)S(1)}, u32[]{:S(2)}, u32[]{:S(2)}) %all-to-all-start.1) | async-done | bytes 1835040 | tf_op jit(solution)/shard_map/while/body/eval_jaxpr/all_to_all | solution.py:81
  366.5 2.5 fusion.72
  369.0 3.7 select_select_fusion.2
  374.7 5.4 %collective-permute-done = bf16[4,8,7168]{2,1,0:T(8,128)(2,1)S(1)} collective-permute-done((bf16[4,8,7168]{2,1,0:T(8,128)(2,1)S(1)}, bf16[4,8,7168]{2,1,0:T(8,128)(2,1)S(1)}, u32[]{:S(2)}, u32[]{:S(2)}) %collective-permute-start) | collective-permute-done | bytes 458784 | tf_op jit(solution)/shard_map/while/body/eval_jaxpr/ppermute | solution.py:13
  384.9 45.1 %all_to_all.24 = bf16[8,16,7168]{2,1,0:T(8,128)(2,1)S(1)} all-to-all(bf16[8,16,7168]{2,1,0:T(8,128)(2,1)S(1)} %bitcast.91), channel_id=1, replica_groups=mesh['section'=4,'ep'=8] {'ep'}, dimensions={0} | all-to-all | bytes 3670016 | tf_op jit(solution)/shard_map/while/body/eval_jaxpr/all_to_all | solution.py:76
  431.1 8.6 %convolution_convert_fusion.3 = bf16[128,7168]{1,0:T(8,128)(2,1)} fusion(bf16[512,7168]{1,0:T(8,128)(2,1)} %get-tuple-element.495, bf16[128,7168]{1,0:T(8,128)(2,1)S(1)} %bitcast.86, bf16[7168,512]{1,0:T(8,128)(2,1)} %get-tuple-element.494, f32[128,512]{1,0:T(8,128)S(1)} %fusion.71), kind=kOutput, calls=%fused_computation.1.clone.1 | convolution fusion | flops 1880358912 | bytes 18612224 | tf_op jit(solution)/shard_map/while/body/eval_jaxpr/dot_general | solution.py:51
  439.8 3.6 all-to-all-start.1
  443.4 42.6 %all-to-all-done.1 = bf16[8,16,7168]{2,1,0:T(8,128)(2,1)S(1)} async-done(((bf16[8,16,7168]{2,1,0:T(8,128)(2,1)}), bf16[8,16,7168]{2,1,0:T(8,128)(2,1)S(1)}, u32[]{:S(2)}, u32[]{:S(2)}) %all-to-all-start.1) | async-done | bytes 1835040 | tf_op jit(solution)/shard_map/while/body/eval_jaxpr/all_to_all | solution.py:81
  488.4 2.5 fusion.72
  490.9 3.7 select_select_fusion.2
  496.5 5.4 %collective-permute-done = bf16[4,8,7168]{2,1,0:T(8,128)(2,1)S(1)} collective-permute-done((bf16[4,8,7168]{2,1,0:T(8,128)(2,1)S(1)}, bf16[4,8,7168]{2,1,0:T(8,128)(2,1)S(1)}, u32[]{:S(2)}, u32[]{:S(2)}) %collective-permute-start) | collective-permute-done | bytes 458784 | tf_op jit(solution)/shard_map/while/body/eval_jaxpr/ppermute | solution.py:13
  (96 shorter events, 45.5 us)
Async XLA Ops:
  1.4 3.4 collective-permute-start.1
  5.5 2.4 collective-permute-start.2
  7.9 3.3 collective-permute-start.3
  13.3 3.2 copy-start.2
  17.7 46.2 %copy-start = (bf16[7168,512]{1,0:T(8,128)(2,1)S(1)}, bf16[7168,512]{1,0:T(8,128)(2,1)}, u32[]{:S(2)}) copy-start(bf16[7168,512]{1,0:T(8,128)(2,1)} %get-tuple-element.493) | copy-start | bytes 22020100 | tf_op jit(solution)/shard_map/while
  73.6 44.4 %all-to-all-start.1 = ((bf16[8,16,7168]{2,1,0:T(8,128)(2,1)}), bf16[8,16,7168]{2,1,0:T(8,128)(2,1)S(1)}, u32[]{:S(2)}, u32[]{:S(2)}) async-start(bf16[8,16,7168]{2,1,0:T(8,128)(2,1)} %bitcast.88), calls=%async_computation.1 | async-start | bytes 3670016 | tf_op jit(solution)/shard_map/while/body/eval_jaxpr/all_to_all | solution.py:81
  126.7 12.4 %collective-permute-start = (bf16[4,8,7168]{2,1,0:T(8,128)(2,1)S(1)}, bf16[4,8,7168]{2,1,0:T(8,128)(2,1)S(1)}, u32[]{:S(2)}, u32[]{:S(2)}) collective-permute-start(bf16[4,8,7168]{2,1,0:T(8,128)(2,1)S(1)} %get-tuple-element.453), channel_id=1, source_target_pairs={{0,8},{8,16},{16,24},{1,9},{9,17},{17,25},{2,10},{10,18},{18,26},{... | collective-permute-start | bytes 1376264 | tf_op jit(solution)/shard_map/while/body/eval_jaxpr/ppermute | solution.py:13
  139.1 3.2 copy-start.2
  143.4 42.8 %copy-start = (bf16[7168,512]{1,0:T(8,128)(2,1)S(1)}, bf16[7168,512]{1,0:T(8,128)(2,1)}, u32[]{:S(2)}) copy-start(bf16[7168,512]{1,0:T(8,128)(2,1)} %get-tuple-element.493) | copy-start | bytes 22020100 | tf_op jit(solution)/shard_map/while
  196.0 46.9 %all-to-all-start.1 = ((bf16[8,16,7168]{2,1,0:T(8,128)(2,1)}), bf16[8,16,7168]{2,1,0:T(8,128)(2,1)S(1)}, u32[]{:S(2)}, u32[]{:S(2)}) async-start(bf16[8,16,7168]{2,1,0:T(8,128)(2,1)} %bitcast.88), calls=%async_computation.1 | async-start | bytes 3670016 | tf_op jit(solution)/shard_map/while/body/eval_jaxpr/all_to_all | solution.py:81
  251.6 7.3 %collective-permute-start = (bf16[4,8,7168]{2,1,0:T(8,128)(2,1)S(1)}, bf16[4,8,7168]{2,1,0:T(8,128)(2,1)S(1)}, u32[]{:S(2)}, u32[]{:S(2)}) collective-permute-start(bf16[4,8,7168]{2,1,0:T(8,128)(2,1)S(1)} %get-tuple-element.453), channel_id=1, source_target_pairs={{0,8},{8,16},{16,24},{1,9},{9,17},{17,25},{2,10},{10,18},{18,26},{... | collective-permute-start | bytes 1376264 | tf_op jit(solution)/shard_map/while/body/eval_jaxpr/ppermute | solution.py:13
  258.9 3.2 copy-start.2
  263.3 44.9 %copy-start = (bf16[7168,512]{1,0:T(8,128)(2,1)S(1)}, bf16[7168,512]{1,0:T(8,128)(2,1)}, u32[]{:S(2)}) copy-start(bf16[7168,512]{1,0:T(8,128)(2,1)} %get-tuple-element.493) | copy-start | bytes 22020100 | tf_op jit(solution)/shard_map/while
  317.9 46.2 %all-to-all-start.1 = ((bf16[8,16,7168]{2,1,0:T(8,128)(2,1)}), bf16[8,16,7168]{2,1,0:T(8,128)(2,1)S(1)}, u32[]{:S(2)}, u32[]{:S(2)}) async-start(bf16[8,16,7168]{2,1,0:T(8,128)(2,1)} %bitcast.88), calls=%async_computation.1 | async-start | bytes 3670016 | tf_op jit(solution)/shard_map/while/body/eval_jaxpr/all_to_all | solution.py:81
  372.7 7.3 %collective-permute-start = (bf16[4,8,7168]{2,1,0:T(8,128)(2,1)S(1)}, bf16[4,8,7168]{2,1,0:T(8,128)(2,1)S(1)}, u32[]{:S(2)}, u32[]{:S(2)}) collective-permute-start(bf16[4,8,7168]{2,1,0:T(8,128)(2,1)S(1)} %get-tuple-element.453), channel_id=1, source_target_pairs={{0,8},{8,16},{16,24},{1,9},{9,17},{17,25},{2,10},{10,18},{18,26},{... | collective-permute-start | bytes 1376264 | tf_op jit(solution)/shard_map/while/body/eval_jaxpr/ppermute | solution.py:13
  380.1 3.2 copy-start.2
  384.4 45.6 %copy-start = (bf16[7168,512]{1,0:T(8,128)(2,1)S(1)}, bf16[7168,512]{1,0:T(8,128)(2,1)}, u32[]{:S(2)}) copy-start(bf16[7168,512]{1,0:T(8,128)(2,1)} %get-tuple-element.493) | copy-start | bytes 22020100 | tf_op jit(solution)/shard_map/while
  439.8 46.2 %all-to-all-start.1 = ((bf16[8,16,7168]{2,1,0:T(8,128)(2,1)}), bf16[8,16,7168]{2,1,0:T(8,128)(2,1)S(1)}, u32[]{:S(2)}, u32[]{:S(2)}) async-start(bf16[8,16,7168]{2,1,0:T(8,128)(2,1)} %bitcast.88), calls=%async_computation.1 | async-start | bytes 3670016 | tf_op jit(solution)/shard_map/while/body/eval_jaxpr/all_to_all | solution.py:81
  494.6 7.3 %collective-permute-start = (bf16[4,8,7168]{2,1,0:T(8,128)(2,1)S(1)}, bf16[4,8,7168]{2,1,0:T(8,128)(2,1)S(1)}, u32[]{:S(2)}, u32[]{:S(2)}) collective-permute-start(bf16[4,8,7168]{2,1,0:T(8,128)(2,1)S(1)} %get-tuple-element.453), channel_id=1, source_target_pairs={{0,8},{8,16},{16,24},{1,9},{9,17},{17,25},{2,10},{10,18},{18,26},{... | collective-permute-start | bytes 1376264 | tf_op jit(solution)/shard_map/while/body/eval_jaxpr/ppermute | solution.py:13
  501.9 0.8 copy-start.1
